TPU v7x, 32 devices: a whole 2x2x4 slice. The times are simulated.
32 devices in a mesh: cols: 32 (over z, y, x, core).
Axes of the slice: x: 2, y: 2, z: 4, core: 2. Of those that a mesh axis runs over, the one named last changes fastest.
Arguments:
- gcm_state: float32 [2, 72, 16384], P(None, None, 'cols'), may hold values from -6 to 6
- crm_state: bfloat16 [2, 58, 32, 16384], P(None, None, None, 'cols'), may hold values from -6 to 6
- span_map: int32 [16384], P('cols'), may hold values from 0 to 16383, as said below
- crm_cost: int32 [16384], P('cols'), may hold values from 1 to 58
- neighbours: int32 [4096, 8], P('cols'), may hold values from -1 to 4095, as said below
Outputs:
- crm_next: bfloat16 [2, 58, 32, 16384], P(None, None, None, 'cols')
- smoothed: float32 [2, 72, 16384], P(None, None, 'cols')
Inputs may be any that keep to these rules, and one draw needn't show every extreme that they name: `span_map`: A permutation of the span positions; position p is held by device p // 512. The columns of each device go, exactly 32 each, to 16 distinct devices, its own among them, and each device receives exactly 32 columns from each of 16 devices. `neighbours`: -1 marks an empty slot and stands only in the last slot; every other entry names an element of the element's own device or of one of the two devices beside it along cols, wrapping around.
All inputs are finite; a program needn't handle non-finite values.
Results may differ from a plain program's by a relative error of at most 0.001.
Values sent between devices are 32-bit elements; how exact they have to be, the bound alone decides.
A program may use at most 128 MiB of HBM per device.

v0:
```python
import jax
import jax.numpy as jnp
from jax import lax
from jax.sharding import PartitionSpec as P

LEV = 72
CRM_LEV = 58
PCOL = 4
NBR = 8
SUBSTEPS = 2


RELAX = 0.5
STEP = 0.5
MIXING = 0.2
LATENT = 0.6
SMOOTHING = 0.5


def padded(shard, sides, width):
    for axis, dim in sides:
        size, length = (lax.axis_size(axis), shard.shape[dim])
        up = [(i, (i + 1) % size) for i in range(size)]
        down = [(j, i) for i, j in up]
        last = lax.slice_in_dim(shard, length - width, length, axis=dim)
        first = lax.slice_in_dim(shard, 0, width, axis=dim)
        before = lax.ppermute(last, axis, up)
        after = lax.ppermute(first, axis, down)
        shard = jnp.concatenate([before, shard, after], axis=dim)
    return shard


def interpolation(rows_out, rows_in):
    target = jnp.arange(rows_out, dtype=jnp.int32)[:, None]
    source = jnp.arange(rows_in, dtype=jnp.int32)[None, :]
    scaled = target * (rows_in - 1)
    lower = scaled // (rows_out - 1)
    weight = (scaled - lower * (rows_out - 1)).astype(jnp.float32) / (rows_out - 1)
    upper = jnp.minimum(lower + 1, rows_in - 1)
    return jnp.where(source == lower, 1.0 - weight, 0.0) + jnp.where(source == upper, weight, 0.0)


def crm_steps(fields, forcing, active):
    levels = fields.shape[1]
    height = jnp.arange(levels, dtype=jnp.float32)
    saturation = (1.0 - 0.8 * height / (levels - 1))[:, None, None]
    for substep in range(SUBSTEPS):
        sideways = jnp.roll(fields, 1, axis=2) + jnp.roll(fields, -1, axis=2) - 2.0 * fields
        upper_cells = jnp.concatenate([fields[:, 1:], fields[:, -1:]], axis=1)
        lower_cells = jnp.concatenate([fields[:, :1], fields[:, :-1]], axis=1)
        vertical = upper_cells + lower_cells - 2.0 * fields
        fields = fields + STEP * (forcing[:, :, None, :] + MIXING * (sideways + vertical))
        condensed = jnp.maximum(fields[1] - saturation, 0.0) * active[:, None, :]
        fields = jnp.stack([fields[0] + LATENT * condensed, fields[1] - condensed])
    return fields


def physics(crm_old, profile, cloud_top):
    start = crm_old.astype(jnp.float32)
    start_mean = jnp.mean(start, axis=2)
    forcing = RELAX * (profile - start_mean)
    levels = crm_old.shape[1]
    active = (jnp.arange(levels, dtype=jnp.int32)[:, None] < cloud_top[None, :]).astype(jnp.float32)
    final = crm_steps(start, forcing, active)
    change = jnp.mean(final, axis=2) - start_mean
    return (final.astype(jnp.bfloat16), change)


def element_mean(values, elements):
    return jnp.mean(values.reshape(2 * LEV, elements, PCOL), axis=2)


def on_device(gcm_state, crm_state, span_map, crm_cost, neighbours):
    devices = lax.axis_size("cols")
    device = lax.axis_index("cols")
    columns = gcm_state.shape[2]
    elements = neighbours.shape[0]
    capacity = 2 * columns // devices
    interp_down = interpolation(CRM_LEV, LEV)
    interp_up = interpolation(LEV, CRM_LEV)
    target = span_map // columns
    span_slot = span_map % columns
    peer_ids = jnp.arange(devices, dtype=jnp.int32)
    onehot = (target[:, None] == peer_ids[None, :]).astype(jnp.int32)
    before = jnp.cumsum(onehot, axis=0) - onehot
    within = jnp.sum(before * onehot, axis=1)
    position = target * capacity + within
    outgoing = gcm_state.reshape(2 * LEV, columns)
    row_count = outgoing.shape[0]
    slot_total = devices * capacity
    send_rows = jnp.zeros((row_count, slot_total), jnp.float32).at[:, position].set(outgoing)
    labels = jnp.stack([span_slot, crm_cost]).astype(jnp.float32)
    empty_labels = jnp.stack(
        [jnp.full((slot_total,), columns, jnp.float32), jnp.zeros((slot_total,), jnp.float32)]
    )
    send_labels = empty_labels.at[:, position].set(labels)
    arrived, arrived_labels = (
        lax.all_to_all(send_rows, "cols", split_axis=1, concat_axis=1, tiled=True),
        lax.all_to_all(send_labels, "cols", split_axis=1, concat_axis=1, tiled=True),
    )
    arrived_slot = arrived_labels[0].astype(jnp.int32)
    placed = (
        jnp.zeros((row_count, columns + 1), jnp.float32)
        .at[:, arrived_slot]
        .set(arrived)[:, :columns]
    )
    span_top = (
        jnp.zeros((columns + 1,), jnp.int32)
        .at[arrived_slot]
        .set(arrived_labels[1].astype(jnp.int32))[:columns]
    )
    span_profile = jnp.einsum(
        "jk,fkc->fjc", interp_down, placed.reshape(2, LEV, columns), precision=lax.Precision.HIGHEST
    )
    crm_next, change = physics(crm_state, span_profile, span_top)
    returning = jnp.einsum(
        "kj,fjc->fkc", interp_up, change, precision=lax.Precision.HIGHEST
    ).reshape(2 * LEV, columns)
    source_slot = jnp.minimum(arrived_slot, columns - 1)
    returned = lax.all_to_all(
        returning[:, source_slot], "cols", split_axis=1, concat_axis=1, tiled=True
    )
    own_rows = returned[:, position]
    tendency = own_rows.reshape(2, LEV, columns)
    updated = gcm_state + tendency
    edge_mean = element_mean(updated, elements)
    extended = padded(edge_mean, (("cols", 1),), elements)
    valid = neighbours >= 0
    offset = jnp.mod(neighbours - (device - 1) * elements, devices * elements)
    lookup = jnp.where(valid, offset, 0)
    gathered = jnp.take(extended, lookup.reshape(-1), axis=1).reshape(2 * LEV, elements, NBR)
    gathered = gathered * valid.astype(jnp.float32)[None]
    neighbour_sum = jnp.sum(gathered, axis=2)
    count = jnp.sum(valid.astype(jnp.float32), axis=1)
    pull = SMOOTHING * (neighbour_sum / count[None, :] - edge_mean)
    smoothed = (updated.reshape(2 * LEV, elements, PCOL) + pull[:, :, None]).reshape(
        2, LEV, columns
    )
    return (crm_next, smoothed)


def solution(mesh):
    placed = (
        P(None, None, "cols"),
        P(None, None, None, "cols"),
        P("cols"),
        P("cols"),
        P("cols", None),
    )
    return jax.shard_map(
        on_device,
        mesh=mesh,
        in_specs=placed,
        out_specs=(P(None, None, None, "cols"), P(None, None, "cols")),
        check_vma=False,
    )
```

profile of v0, /device:TPU:0, one launch (start us, length us, event | category | flops | bytes accessed | tf_op | source)
XLA Modules:
  0.0 169.9 jit_solution(7699775522284530339)
XLA Ops:
  0.6 0.7 add_select_fusion.1
  1.3 1.2 reduce-window.6
  2.9 0.7 fusion.67
  3.7 1.0 copy.42
  4.8 1.9 %scatter_fusion = f32[2,1024]{0,1:T(8,128)S(1)} fusion(f32[2,1024]{0,1:T(8,128)S(1)} %copy.42, s32[512]{0:T(512)S(1)} %compare_select_fusion.4, f32[512,2]{1,0:T(8,128)S(1)} %copy.27), kind=kCustom, calls=%fused_computation.3 | custom fusion | bytes 14336 | tf_op jit(solution)/shard_map/scatter | solution.py:96
  6.7 0.9 copy.28
  7.6 7.3 %all-to-all-start = ((f32[2,32,32]{2,0,1:T(2,128)}), f32[2,32,32]{2,0,1:T(2,128)S(1)}, u32[]{:S(2)}, u32[]{:S(2)}) async-start(f32[2,32,32]{2,0,1:T(2,128)} %copy.28), calls=%async_computation | async-start | bytes 65536 | tf_op jit(solution)/shard_map/all_to_all | solution.py:99
  14.9 11.3 %fusion.79 = (f32[2,58,31,512]{3,2,1,0:T(8,128)}, f32[2,58,31,512]{3,2,1,0:T(8,128)}) fusion(bf16[2,58,32,512]{3,2,1,0:T(8,128)(2,1)} %param.6), kind=kLoop, calls=%fused_computation.161 | loop fusion | bytes 29458432 | tf_op jit(solution)/shard_map/jit(_roll_static)/slice | solution.py:48
  26.2 7.3 %fusion.78 = (f32[2,57,32,512]{3,2,1,0:T(8,128)}, f32[2,57,32,512]{3,2,1,0:T(8,128)}) fusion(bf16[2,58,32,512]{3,2,1,0:T(8,128)(2,1)S(1)} %copy-done), kind=kLoop, calls=%fused_computation.160 | loop fusion | bytes 29884416 | tf_op jit(solution)/shard_map/slice | solution.py:50
  34.1 3.3 %scatter_custom_fusion.1 = f32[144,1024]{0,1:T(8,128)} fusion(s32[512]{0:T(512)S(1)} %compare_select_fusion.4, f32[144,512]{0,1:T(8,128)S(1)} %copy.29, f32[]{:T(128)} %constant.56.clone.1), kind=kCustom, calls=%fused_computation.62 | custom fusion | bytes 1114116 | tf_op jit(solution)/shard_map/scatter | solution.py:91
  37.4 5.8 %all-to-all-start.1 = ((f32[144,32,32]{0,2,1:T(8,128)}), f32[144,32,32]{0,2,1:T(8,128)S(1)}, u32[]{:S(2)}, u32[]{:S(2)}) async-start(f32[144,32,32]{0,2,1:T(8,128)} %bitcast.9), calls=%async_computation.1 | async-start | bytes 2097152 | tf_op jit(solution)/shard_map/all_to_all | solution.py:98
  43.3 3.4 %convert_reduce_fusion = f32[2,58,512]{2,1,0:T(8,128)S(1)} fusion(bf16[2,58,32,512]{3,2,1,0:T(8,128)(2,1)} %param.6), kind=kLoop, calls=%fused_computation.55 | loop fusion | flops 3741696 | bytes 4038656 | tf_op jit(solution)/shard_map/reduce_sum | solution.py:60
  46.9 4.3 %scatter_custom_fusion.3 = s32[513]{0:T(1024)S(1)} fusion(s32[1024]{0:T(1024)S(1)} %bitcast.83, s32[1024]{0:T(1024)S(1)} %reshape.308, s32[]{:T(128)} %constant.62.clone.1), kind=kCustom, calls=%fused_computation.139 | custom fusion | bytes 2056 | tf_op jit(solution)/shard_map/scatter | solution.py:110
  51.3 18.2 %all-to-all-done.1 = f32[144,32,32]{0,2,1:T(8,128)S(1)} async-done(((f32[144,32,32]{0,2,1:T(8,128)}), f32[144,32,32]{0,2,1:T(8,128)S(1)}, u32[]{:S(2)}, u32[]{:S(2)}) %all-to-all-start.1) | async-done | bytes 589856 | tf_op jit(solution)/shard_map/all_to_all | solution.py:98
  69.5 5.1 %scatter_custom_fusion.2 = f32[144,513]{0,1:T(8,128)S(1)} fusion(s32[1024]{0:T(1024)S(1)} %bitcast.84, f32[1024,144]{1,0:T(8,128)S(1)} %bitcast.78, f32[]{:T(128)} %constant.56.clone.1), kind=kCustom, calls=%fused_computation.66 | custom fusion | bytes 295492 | tf_op jit(solution)/shard_map/scatter | solution.py:105
  75.2 13.5 %fusion.7 = f32[2,58,32,512]{3,2,1,0:T(8,128)S(1)} fusion(f32[2,58,31,512]{3,2,1,0:T(8,128)} %get-tuple-element.23, f32[2,58,1,512]{3,2,1,0:T(1,128)S(1)} %get-tuple-element.25, f32[2,58,1,512]{3,2,1,0:T(1,128)S(1)} %get-tuple-element.24, f32[2,58,31,512]{3,2,1,0:T(8,128)} %get-tuple-element.22, f32[2,1,32,512]{3,2,1,0:T(8,128)S(1)} %get-tuple-element.19, ...), kind=kLoop, calls=%fused_computation.32 | loop fusion | flops 28508160 | bytes 42049536 | tf_op jit(solution)/shard_map/add | solution.py:52
  88.8 1.5 fusion.21
  90.3 6.1 %fusion.17 = (f32[2,57,32,512]{3,2,1,0:T(8,128)}, f32[2,57,32,512]{3,2,1,0:T(8,128)}) fusion(f32[1,58,32,512]{3,2,1,0:T(8,128)S(1)} %get-tuple-element.9, f32[1,58,32,512]{3,2,1,0:T(8,128)S(1)} %get-tuple-element.8), kind=kLoop, calls=%fused_computation.46 | loop fusion | flops 3735552 | bytes 22544384 | tf_op jit(solution)/shard_map/stack | solution.py:54
  96.8 4.0 %fusion.1 = (f32[2,58,31,512]{3,2,1,0:T(8,128)S(1)}, f32[2,58,31,512]{3,2,1,0:T(8,128)}) fusion(f32[1,58,32,512]{3,2,1,0:T(8,128)S(1)} %get-tuple-element.9, f32[1,58,32,512]{3,2,1,0:T(8,128)S(1)} %get-tuple-element.8), kind=kLoop, calls=%fused_computation.25 | loop fusion | flops 3682304 | bytes 22331392 | tf_op jit(solution)/shard_map/stack | solution.py:54
  100.9 9.7 %fusion.14 = f32[2,58,32,512]{3,2,1,0:T(8,128)S(1)} fusion(f32[2,58,31,512]{3,2,1,0:T(8,128)} %get-tuple-element.15, f32[2,58,1,512]{3,2,1,0:T(1,128)S(1)} %get-tuple-element.17, f32[2,58,1,512]{3,2,1,0:T(1,128)S(1)} %get-tuple-element.16, f32[2,58,31,512]{3,2,1,0:T(8,128)S(1)} %get-tuple-element.14, f32[1,58,32,512]{3,2,1,0:T(8,128)S(1)} %get-tuple-element.8, ...), kind=kLoop, calls=%fused_computation.41 | loop fusion | flops 28508160 | bytes 45850624 | tf_op jit(solution)/shard_map/add | solution.py:52
  110.5 1.9 %slice_add_fusion = (f32[1,58,32,512]{3,2,1,0:T(8,128)S(1)}, f32[1,58,32,512]{3,2,1,0:T(8,128)S(1)}) fusion(f32[2,58,32,512]{3,2,1,0:T(8,128)S(1)} %fusion.14, f32[58,512]{1,0:T(8,128)S(1)} %fusion.40, f32[58]{0:T(128)S(1)} %multiply_subtract_fusion), kind=kLoop, calls=%fused_computation.49 | loop fusion | flops 5701632 | bytes 15323368 | tf_op jit(solution)/shard_map/add | solution.py:54
  112.5 1.5 fusion.18
  114.5 0.9 copy-done.2
  115.6 4.7 %gather_fusion = f32[1024,144]{1,0:T(8,128)} fusion(f32[144,512]{0,1:T(8,128)S(1)} %copy.31, s32[1024]{0:T(1024)S(1)} %broadcast_clamp_fusion.1), kind=kCustom, calls=%fused_computation | custom fusion | bytes 1183744 | tf_op jit(solution)/shard_map/gather | solution.py:121
  120.3 3.8 %all-to-all-start.2 = ((f32[144,32,32]{0,2,1:T(8,128)}), f32[144,32,32]{0,2,1:T(8,128)S(1)}, u32[]{:S(2)}, u32[]{:S(2)}) async-start(f32[144,32,32]{0,2,1:T(8,128)} %bitcast.20), calls=%async_computation.2 | async-start | bytes 2097152 | tf_op jit(solution)/shard_map/all_to_all | solution.py:120
  124.6 25.5 %all-to-all-done.2 = f32[144,32,32]{0,2,1:T(8,128)S(1)} async-done(((f32[144,32,32]{0,2,1:T(8,128)}), f32[144,32,32]{0,2,1:T(8,128)S(1)}, u32[]{:S(2)}, u32[]{:S(2)}) %all-to-all-start.2) | async-done | bytes 589856 | tf_op jit(solution)/shard_map/all_to_all | solution.py:120
  150.1 1.6 gather_fusion.1
  153.0 5.3 %collective-permute-start.1 = (f32[144,128]{0,1:T(8,128)S(1)}, f32[144,128]{0,1:T(8,128)S(1)}, u32[]{:S(2)}, u32[]{:S(2)}) collective-permute-start(f32[144,128]{0,1:T(8,128)S(1)} %broadcast_multiply_fusion), channel_id=1, source_target_pairs={{1,0},{2,1},{3,2},{4,3},{5,4},{6,5},{7,6},{8,7},{9,8},{10,9},{11,1... | collective-permute-start | bytes 221192 | tf_op jit(solution)/shard_map/ppermute | solution.py:28
  158.4 5.8 %fusion.19 = bf16[2,58,32,512]{3,2,1,0:T(8,128)(2,1)} fusion(f32[1,58,32,512]{3,2,1,0:T(8,128)} %copy-done.2, f32[1,58,32,512]{3,2,1,0:T(8,128)} %copy-done.1), kind=kLoop, calls=%fused_computation.48 | loop fusion | flops 1900544 | bytes 11403264 | tf_op jit(solution)/shard_map/convert_element_type | solution.py:66
  164.2 3.5 %gather_fusion.2 = f32[1024,144]{1,0:T(8,128)S(1)} fusion(f32[144,384]{0,1:T(8,128)S(1)} %pad_maximum_fusion.2, s32[1024]{0:T(1024)S(1)} %broadcast_clamp_fusion), kind=kCustom, calls=%fused_computation.2 | custom fusion | bytes 1183744 | tf_op jit(solution)/shard_map/jit(_take)/gather | solution.py:131
  167.6 0.7 fusion.25
  169.2 0.8 add.213
  (62 shorter events, 5.9 us)
Async XLA Ops:
  7.6 29.8 %all-to-all-start = ((f32[2,32,32]{2,0,1:T(2,128)}), f32[2,32,32]{2,0,1:T(2,128)S(1)}, u32[]{:S(2)}, u32[]{:S(2)}) async-start(f32[2,32,32]{2,0,1:T(2,128)} %copy.28), calls=%async_computation | async-start | bytes 65536 | tf_op jit(solution)/shard_map/all_to_all | solution.py:99
  14.9 11.3 %copy-start = (bf16[2,58,32,512]{3,2,1,0:T(8,128)(2,1)S(1)}, bf16[2,58,32,512]{3,2,1,0:T(8,128)(2,1)}, u32[]{:S(2)}) copy-start(bf16[2,58,32,512]{3,2,1,0:T(8,128)(2,1)} %param.6) | copy-start | bytes 11403268
  26.2 7.7 %copy-start.3 = (f32[2,72,512]{2,1,0:T(8,128)S(1)}, f32[2,72,512]{2,1,0:T(8,128)}, u32[]{:S(2)}) copy-start(f32[2,72,512]{2,1,0:T(8,128)} %param.5) | copy-start | bytes 884740
  37.4 32.1 %all-to-all-start.1 = ((f32[144,32,32]{0,2,1:T(8,128)}), f32[144,32,32]{0,2,1:T(8,128)S(1)}, u32[]{:S(2)}, u32[]{:S(2)}) async-start(f32[144,32,32]{0,2,1:T(8,128)} %bitcast.9), calls=%async_computation.1 | async-start | bytes 2097152 | tf_op jit(solution)/shard_map/all_to_all | solution.py:98
  112.4 2.0 %copy-start.1 = (f32[1,58,32,512]{3,2,1,0:T(8,128)}, f32[1,58,32,512]{3,2,1,0:T(8,128)S(1)}, u32[]{:S(2)}) copy-start(f32[1,58,32,512]{3,2,1,0:T(8,128)S(1)} %get-tuple-element.6) | copy-start | bytes 11403268
  112.5 2.9 %copy-start.2 = (f32[1,58,32,512]{3,2,1,0:T(8,128)}, f32[1,58,32,512]{3,2,1,0:T(8,128)S(1)}, u32[]{:S(2)}) copy-start(f32[1,58,32,512]{3,2,1,0:T(8,128)S(1)} %get-tuple-element.7) | copy-start | bytes 11403268
  112.5 11.7 %copy-start.4 = (s32[128,8]{0,1:T(8,128)S(1)}, s32[128,8]{0,1:T(8,128)}, u32[]{:S(2)}) copy-start(s32[128,8]{0,1:T(8,128)} %param.9) | copy-start | bytes 12292
  120.3 29.9 %all-to-all-start.2 = ((f32[144,32,32]{0,2,1:T(8,128)}), f32[144,32,32]{0,2,1:T(8,128)S(1)}, u32[]{:S(2)}, u32[]{:S(2)}) async-start(f32[144,32,32]{0,2,1:T(8,128)} %bitcast.20), calls=%async_computation.2 | async-start | bytes 2097152 | tf_op jit(solution)/shard_map/all_to_all | solution.py:120
  153.0 11.2 %collective-permute-start = (f32[144,128]{0,1:T(8,128)S(1)}, f32[144,128]{0,1:T(8,128)S(1)}, u32[]{:S(2)}, u32[]{:S(2)}) collective-permute-start(f32[144,128]{0,1:T(8,128)S(1)} %broadcast_multiply_fusion), channel_id=1, source_target_pairs={{0,1},{1,2},{2,3},{3,4},{4,5},{5,6},{6,7},{7,8},{8,9},{9,10},{10,1... | collective-permute-start | bytes 221192 | tf_op jit(solution)/shard_map/ppermute | solution.py:27
  153.0 11.1 %collective-permute-start.1 = (f32[144,128]{0,1:T(8,128)S(1)}, f32[144,128]{0,1:T(8,128)S(1)}, u32[]{:S(2)}, u32[]{:S(2)}) collective-permute-start(f32[144,128]{0,1:T(8,128)S(1)} %broadcast_multiply_fusion), channel_id=1, source_target_pairs={{1,0},{2,1},{3,2},{4,3},{5,4},{6,5},{7,6},{8,7},{9,8},{10,9},{11,1... | collective-permute-start | bytes 221192 | tf_op jit(solution)/shard_map/ppermute | solution.py:28
where the time goes:
time: 170 us
  other arithmetic  52.7 us (31%)
  local copies, waits for them, and re-layouts  49.2 us (29%)
  waiting for transfers between devices  43.7 us (26%)
  starting transfers between devices  22.3 us (13%)
    all_to_all x1, waiting for transfers between devices, on_device(): lax.all_to_all(returning[:, source_slot], 'cols', split_axis=1, concat_ax...  25.5 us
    add x2, other arithmetic, crm_steps(): fields + STEP * (forcing[:, :, None, :] + MIXING * (sideways + vertical))  23.2 us
    all_to_all x1, waiting for transfers between devices, on_device(): lax.all_to_all(send_rows, 'cols', split_axis=1, concat_axis=1, tiled=True)  18.2 us
    slice x2, local copies, waits for them, and re-layouts, crm_steps(): jnp.roll(fields, -1, axis=2)  11.6 us
    another operation x4, other arithmetic, crm_steps(): fields = jnp.stack([fields[0] + LATENT * condensed, fields[1] - condensed])  10.6 us
    slice x2, local copies, waits for them, and re-layouts, crm_steps(): lower_cells = jnp.concatenate([fields[:, :1], fields[:, :-1]], axis=1)  7.31 us
    all_to_all x1, starting transfers between devices, on_device(): lax.all_to_all(send_labels, 'cols', split_axis=1, concat_axis=1, tiled=True)  7.3 us
    all_to_all x1, starting transfers between devices, on_device(): lax.all_to_all(send_rows, 'cols', split_axis=1, concat_axis=1, tiled=True)  5.83 us
  transfers between devices with their start and end apart: 5, of which 2 were waited for; matrix products, arithmetic and copies ran while one was open for 22% of the time, Pallas kernels for 0%

commit v1 on v0

v1 whole, which is shorter than its diff:
```python
import functools

import numpy as np
import jax
import jax.numpy as jnp
from jax import lax
from jax.experimental import pallas as pl
from jax.experimental.pallas import tpu as pltpu
from jax.sharding import PartitionSpec as P

LEV = 72
CRM_NX = 32
CRM_LEV = 58
PCOL = 4
NBR = 8
FEATURES = 2 * CRM_LEV
WIDTH = 128
CHUNK = 256

RELAX = 0.5
STEP = 0.5
MIXING = 0.2
LATENT = 0.6
SMOOTHING = 0.5

MESH = pl.DeviceIdType.MESH
F32 = jnp.float32
BF16 = jnp.bfloat16


def interpolation(rows_out, rows_in):
    target = np.arange(rows_out, dtype=np.int32)[:, None]
    source = np.arange(rows_in, dtype=np.int32)[None, :]
    scaled = target * (rows_in - 1)
    lower = scaled // (rows_out - 1)
    weight = (scaled - lower * (rows_out - 1)).astype(np.float32) / np.float32(rows_out - 1)
    upper = np.minimum(lower + 1, rows_in - 1)
    zero = np.float32(0.0)
    return np.where(source == lower, np.float32(1.0) - weight, zero) + np.where(
        source == upper, weight, zero
    )


def both_fields(rows_out, rows_in, height, width):
    matrix = np.zeros((height, width), np.float32)
    block = interpolation(rows_out, rows_in)
    matrix[:rows_out, :rows_in] = block
    matrix[rows_out : 2 * rows_out, rows_in : 2 * rows_in] = block
    return matrix


def halves(values):
    high = values.astype(BF16)
    low = (values - high.astype(F32)).astype(BF16)
    return high, low


def dot(a, b, dims):
    return lax.dot_general(a, b, (dims, ((), ())), preferred_element_type=F32)


AB = ((1,), (0,))
ABT = ((1,), (1,))


def split_dot(values, chosen, dims):
    rows = values.shape[0]
    both = dot(jnp.concatenate(halves(values), axis=0), chosen, dims)
    return both[:rows] + both[rows:]


def onehot(mask):
    return jnp.where(mask, 1.0, 0.0).astype(BF16)


def kernel(
    devices,
    gcm_ref,
    crm_ref,
    span_ref,
    cost_ref,
    near_ref,
    down_ref,
    up_ref,
    next_ref,
    smooth_ref,
    crm_buf,
    fields,
    next_buf,
    pick_out,
    pick_in,
    sent,
    arrived,
    sent_back,
    arrived_back,
    start_mean,
    forcing,
    change,
    own_mean,
    near_mean,
    near_pick,
    load_sem,
    store_sem,
    out_send,
    out_recv,
    back_send,
    back_recv,
    near_send,
    near_recv,
):
    me = lax.axis_index("cols")
    columns = gcm_ref.shape[1]
    elements = near_ref.shape[0]
    capacity = sent.shape[1]
    slots = devices * capacity
    column_bits = columns.bit_length() - 1

    barrier = pltpu.get_barrier_semaphore()

    def greet(k, carry):
        pl.semaphore_signal(
            barrier, inc=1, device_id=(lax.rem(me + k, devices),), device_id_type=MESH
        )
        return carry

    lax.fori_loop(1, devices, greet, 0)

    load = pltpu.make_async_copy(crm_ref, crm_buf.at[:, pl.ds(1, CRM_LEV)], load_sem)
    load.start()

    span = span_ref[...]
    target = lax.shift_right_logical(span, column_bits)
    place = jnp.bitwise_and(span, columns - 1)
    peers = lax.broadcasted_iota(jnp.int32, (devices, columns), 0)
    mine = peers == target
    first = lax.broadcasted_iota(jnp.int32, (columns, columns), 0)
    second = lax.broadcasted_iota(jnp.int32, (columns, columns), 1)
    before = dot(onehot(mine), onehot(first < second), AB)
    slot = before + (peers * capacity).astype(F32)
    position = jnp.sum(jnp.where(mine, slot, 0.0), axis=0, keepdims=True).astype(jnp.int32)

    profile = lax.dot_general(
        down_ref[...],
        gcm_ref[...],
        (AB, ((), ())),
        precision=lax.Precision.HIGHEST,
        preferred_element_type=F32,
    )
    row = lax.broadcasted_iota(jnp.int32, (WIDTH, columns), 0)
    message = jnp.where(row == FEATURES, (place + 1).astype(F32), profile)
    message = jnp.where(row == FEATURES + 1, cost_ref[...].astype(F32), message)
    message_parts = jnp.concatenate(halves(message), axis=0)

    peers_chunk = CHUNK // capacity
    for chunk in range(slots // CHUNK):
        index = lax.broadcasted_iota(jnp.int32, (CHUNK, columns), 0) + chunk * CHUNK
        chosen = onehot(index == position)
        pick_out[chunk * CHUNK : (chunk + 1) * CHUNK, :] = chosen
        packed = dot(chosen, message_parts, ABT)
        packed = packed[:, :WIDTH] + packed[:, WIDTH:]
        sent[chunk * peers_chunk : (chunk + 1) * peers_chunk] = packed.reshape(
            peers_chunk, capacity, WIDTH
        )

    pl.semaphore_wait(barrier, devices - 1)

    def relay(source, landing, send_sem, recv_sem):
        def send(k, carry):
            peer = lax.rem(me + k, devices)
            pltpu.make_async_remote_copy(
                src_ref=source.at[peer],
                dst_ref=landing.at[me],
                send_sem=send_sem,
                recv_sem=recv_sem,
                device_id=(peer,),
                device_id_type=MESH,
            ).start()
            return carry

        lax.fori_loop(1, devices, send, 0)
        landing[me] = source[me]
        return pltpu.make_async_remote_copy(
            src_ref=source.at[pl.ds(0, devices - 1)],
            dst_ref=landing.at[pl.ds(0, devices - 1)],
            send_sem=send_sem,
            recv_sem=recv_sem,
            device_id=(lax.rem(me + 1, devices),),
            device_id_type=MESH,
        )

    outward = relay(sent, arrived, out_send, out_recv)

    load.wait()
    for field in range(2):
        crm_buf[field, 0] = crm_buf[field, 1]
        crm_buf[field, CRM_LEV + 1] = crm_buf[field, CRM_LEV]

    def stencil(here, above, below):
        sideways = pltpu.roll(here, 1, 0) + pltpu.roll(here, CRM_NX - 1, 0)
        return here + (STEP * MIXING) * ((sideways + (above + below)) - 4.0 * here)

    def prepare(j, carry):
        for field in range(2):
            here = crm_buf[field, j + 1].astype(F32)
            above = crm_buf[field, j + 2].astype(F32)
            below = crm_buf[field, j].astype(F32)
            fields[field, j + 1] = stencil(here, above, below)
            start_mean[pl.ds(field * CRM_LEV + j, 1), :] = jnp.sum(
                here, axis=0, keepdims=True
            ) * (1.0 / CRM_NX)
        return carry

    lax.fori_loop(0, CRM_LEV, prepare, 0)

    near = near_ref[...]
    total = devices * elements
    offset = near - (me - 1) * elements
    offset = jnp.where(offset < 0, offset + total, offset)
    offset = jnp.where(offset >= total, offset - total, offset)
    offset = jnp.where(near >= 0, offset, -1)
    spots = lax.broadcasted_iota(jnp.int32, (elements, 3 * elements), 1)
    chosen = jnp.zeros((elements, 3 * elements), F32)
    for s in range(NBR):
        chosen = chosen + jnp.where(offset[:, s : s + 1] == spots, 1.0, 0.0)
    near_pick[...] = chosen.astype(BF16)

    outward.wait_recv()
    landed = arrived[...].reshape(slots, WIDTH)
    labels = landed[:, FEATURES : FEATURES + 1].astype(jnp.int32)
    columns_at = lax.broadcasted_iota(jnp.int32, (slots, columns), 1) + 1
    pick_in[...] = onehot(labels == columns_at)
    placed = split_dot(landed.T, pick_in[...], AB)
    top = placed[FEATURES + 1 : FEATURES + 2, :]
    forcing[...] = (STEP * RELAX) * (placed[:FEATURES] - start_mean[...])

    def condense(j, heat, moisture):
        level = j.astype(F32)
        saturation = 1.0 - 0.8 * level / (CRM_LEV - 1)
        active = jnp.where(level < top, 1.0, 0.0)
        condensed = jnp.maximum(moisture - saturation, 0.0) * active
        return heat + LATENT * condensed, moisture - condensed

    def push(j):
        return forcing[pl.ds(j, 1), :], forcing[pl.ds(CRM_LEV + j, 1), :]

    def first_step(j, carry):
        push0, push1 = push(j)
        heat, moisture = condense(j, fields[0, j + 1] + push0, fields[1, j + 1] + push1)
        fields[0, j + 1] = heat
        fields[1, j + 1] = moisture
        return carry

    lax.fori_loop(0, CRM_LEV, first_step, 0)
    for field in range(2):
        fields[field, 0] = fields[field, 1]
        fields[field, CRM_LEV + 1] = fields[field, CRM_LEV]

    change[FEATURES:, :] = jnp.zeros((WIDTH - FEATURES, columns), F32)

    def second_step(j, carry):
        push0, push1 = push(j)
        heat = stencil(fields[0, j + 1], fields[0, j + 2], fields[0, j]) + push0
        moisture = stencil(fields[1, j + 1], fields[1, j + 2], fields[1, j]) + push1
        heat, moisture = condense(j, heat, moisture)
        for field, final in ((0, heat), (1, moisture)):
            next_buf[field, j] = final.astype(BF16)
            at = pl.ds(field * CRM_LEV + j, 1)
            change[at, :] = (
                jnp.sum(final, axis=0, keepdims=True) * (1.0 / CRM_NX) - start_mean[at, :]
            )
        return carry

    lax.fori_loop(0, CRM_LEV, second_step, 0)

    change_parts = jnp.concatenate(halves(change[...]), axis=0)
    for chunk in range(slots // CHUNK):
        packed = dot(pick_in[chunk * CHUNK : (chunk + 1) * CHUNK, :], change_parts, ABT)
        packed = packed[:, :WIDTH] + packed[:, WIDTH:]
        sent_back[chunk * peers_chunk : (chunk + 1) * peers_chunk] = packed.reshape(
            peers_chunk, capacity, WIDTH
        )
    inward = relay(sent_back, arrived_back, back_send, back_recv)
    store = pltpu.make_async_copy(next_buf, next_ref, store_sem)
    store.start()

    inward.wait_recv()
    own = split_dot(arrived_back[...].reshape(slots, WIDTH).T, pick_out[...], AB)
    tendency = lax.dot_general(
        up_ref[...],
        own,
        (AB, ((), ())),
        precision=lax.Precision.HIGHEST,
        preferred_element_type=F32,
    )
    updated = gcm_ref[...] + tendency
    member = lax.broadcasted_iota(jnp.int32, (elements, columns), 1)
    lowest = lax.broadcasted_iota(jnp.int32, (elements, columns), 0) * PCOL
    inside = onehot((member >= lowest) & (member < lowest + PCOL))
    own_mean[...] = split_dot(updated, inside, ABT) * (1.0 / PCOL)

    exchanges = []
    for side in range(2):
        peer = lax.rem(me + 1, devices) if side == 0 else lax.rem(me + devices - 1, devices)
        exchange = pltpu.make_async_remote_copy(
            src_ref=own_mean,
            dst_ref=near_mean.at[side],
            send_sem=near_send.at[side],
            recv_sem=near_recv.at[side],
            device_id=(peer,),
            device_id_type=MESH,
        )
        exchange.start()
        exchanges.append(exchange)
    edge_mean = own_mean[...]
    ones = jnp.ones((8, 3 * elements), BF16)
    count = dot(ones, near_pick[...], ABT)[:1]
    scale = 1.0 / count
    total_near = split_dot(edge_mean, near_pick[:, elements : 2 * elements], ABT)
    for side in range(2):
        exchanges[side].wait_recv()
        spot = 2 * side * elements
        total_near = total_near + split_dot(
            near_mean[side], near_pick[:, spot : spot + elements], ABT
        )
    pull = SMOOTHING * (total_near * scale - edge_mean)
    smooth_ref[...] = updated + split_dot(pull, inside, AB)

    outward.wait_send()
    inward.wait_send()
    for exchange in exchanges:
        exchange.wait_send()
    store.wait()


def on_device(devices, gcm_state, crm_state, span_map, crm_cost, neighbours):
    columns = gcm_state.shape[2]
    elements = neighbours.shape[0]
    capacity = 2 * columns // devices
    slots = devices * capacity
    down = jnp.asarray(both_fields(CRM_LEV, LEV, WIDTH, 2 * LEV))
    up = jnp.asarray(both_fields(LEV, CRM_LEV, 2 * LEV, WIDTH))
    vmem = pl.BlockSpec(memory_space=pltpu.VMEM)
    anywhere = pl.BlockSpec(memory_space=pl.ANY)
    relay = pltpu.VMEM((devices, capacity, WIDTH), F32)
    crm_next, smoothed = pl.pallas_call(
        functools.partial(kernel, devices),
        out_shape=(
            jax.ShapeDtypeStruct(crm_state.shape, BF16),
            jax.ShapeDtypeStruct((2 * LEV, columns), F32),
        ),
        in_specs=[vmem, anywhere, vmem, vmem, vmem, vmem, vmem],
        out_specs=(anywhere, vmem),
        scratch_shapes=[
            pltpu.VMEM((2, CRM_LEV + 2, CRM_NX, columns), BF16),
            pltpu.VMEM((2, CRM_LEV + 2, CRM_NX, columns), F32),
            pltpu.VMEM((2, CRM_LEV, CRM_NX, columns), BF16),
            pltpu.VMEM((slots, columns), BF16),
            pltpu.VMEM((slots, columns), BF16),
            relay,
            relay,
            relay,
            relay,
            pltpu.VMEM((FEATURES, columns), F32),
            pltpu.VMEM((FEATURES, columns), F32),
            pltpu.VMEM((WIDTH, columns), F32),
            pltpu.VMEM((2 * LEV, elements), F32),
            pltpu.VMEM((2, 2 * LEV, elements), F32),
            pltpu.VMEM((elements, 3 * elements), BF16),
            pltpu.SemaphoreType.DMA,
            pltpu.SemaphoreType.DMA,
            pltpu.SemaphoreType.DMA,
            pltpu.SemaphoreType.DMA,
            pltpu.SemaphoreType.DMA,
            pltpu.SemaphoreType.DMA,
            pltpu.SemaphoreType.DMA((2,)),
            pltpu.SemaphoreType.DMA((2,)),
        ],
        compiler_params=pltpu.CompilerParams(
            collective_id=0, has_side_effects=True, vmem_limit_bytes=60 * 1024 * 1024
        ),
    )(
        gcm_state.reshape(2 * LEV, columns),
        crm_state,
        span_map.reshape(1, columns),
        crm_cost.reshape(1, columns),
        neighbours,
        down,
        up,
    )
    return crm_next, smoothed.reshape(2, LEV, columns)


def solution(mesh):
    placed = (
        P(None, None, "cols"),
        P(None, None, None, "cols"),
        P("cols"),
        P("cols"),
        P("cols", None),
    )
    return jax.shard_map(
        functools.partial(on_device, mesh.shape["cols"]),
        mesh=mesh,
        in_specs=placed,
        out_specs=(P(None, None, None, "cols"), P(None, None, "cols")),
        check_vma=False,
    )
```

time: 170 us -> 58 us (0.34)
  other arithmetic: 52.7 us -> 0 us
  Pallas kernels: 0 us -> 50.5 us
  waiting for transfers between devices: 43.7 us -> 0 us
  local copies, waits for them, and re-layouts: 49.2 us -> 6.66 us
  starting transfers between devices: 22.3 us -> 0 us
    pallas_call x0 -> x1, Pallas kernels: none -> 50.5 us  [on_device(): pl.pallas_call(functools.partial(kernel, devices), out_shape=(jax.ShapeDt...]
    all_to_all x3 -> x0, waiting for transfers between devices: 43.7 us -> none  [the longest x1 25.5 us: on_device(): lax.all_to_all(returning[:, source_slot], 'cols', split_axis=1, concat_ax...]
    add x5 -> x0, other arithmetic: 25.9 us -> none  [the longest x2 23.2 us: crm_steps(): fields + STEP * (forcing[:, :, None, :] + MIXING * (sideways + vertical))]
    slice x7 -> x0, local copies, waits for them, and re-layouts: 19.1 us -> none  [the longest x2 11.6 us: crm_steps(): jnp.roll(fields, -1, axis=2)]
    all_to_all x3 -> x0, starting transfers between devices: 17 us -> none  [the longest x1 7.3 us: on_device(): lax.all_to_all(send_labels, 'cols', split_axis=1, concat_axis=1, tiled=True)]
    scatter x4 -> x0, local copies, waits for them, and re-layouts: 14.6 us -> none  [the longest x1 5.07 us: on_device(): placed = jnp.zeros((row_count, columns + 1), jnp.float32).at[:, arrived_s...]
    another operation x6 -> x0, other arithmetic: 11.8 us -> none  [the longest x4 10.6 us: crm_steps(): fields = jnp.stack([fields[0] + LATENT * condensed, fields[1] - condensed])]
    gather x4 -> x0, local copies, waits for them, and re-layouts: 9.88 us -> none  [the longest x1 4.68 us: on_device(): returning[:, source_slot]]
  transfers between devices with their start and end apart: 5 -> 0, of which waited for: 2 -> 0; matrix products, arithmetic and copies ran while one was open for 22% -> 0% of each run, Pallas kernels for 0% -> 0%
where the time goes in v1:
time: 58 us; the launch traced here: 57.8 us
  Pallas kernels  50.5 us (87%)
  local copies, waits for them, and re-layouts  6.66 us (11%)
  between operations  0.65 us (1%)
    pallas_call x1, Pallas kernels, on_device(): pl.pallas_call(functools.partial(kernel, devices), out_shape=(jax.ShapeDt...  50.5 us
    unnamed x5, local copies, waits for them, and re-layouts  6.66 us

profile of v1, /device:TPU:0, one launch (start us, length us, event | category | flops | bytes accessed | tf_op | source)
XLA Modules:
  0.0 57.8 jit_solution(3430751616265293356)
XLA Ops:
  0.6 1.4 %copy.9.near_ref = s32[128,8]{1,0:T(8,128)} copy(s32[128,8]{0,1:T(8,128)} %param.11) | data formatting | bytes 8192 | tf_op args[4]
  2.0 50.5 %shard_map.86 = (bf16[2,58,32,512]{3,2,1,0:T(8,128)(2,1)}, f32[144,512]{1,0:T(8,128)}) custom-call(f32[144,512]{1,0:T(8,128)} %bitcast.4, bf16[2,58,32,512]{3,2,1,0:T(8,128)(2,1)} %crm_ref.1, s32[1,512]{1,0:T(1,128)} %bitcast.6, s32[1,512]{1,0:T(1,128)} %bitcast.7, s32[128,8]{1,0:T(8,128)} %copy.9.near_ref, f32[128,144]{1,0:T(8,128)} %constant.4.clone.down_ref, ...), custom_call_target="tpu_custom_call" | custom-call | tf_op jit(solution)/shard_map/pallas_call | solution.py:345
  52.6 0.0 copy-start
  52.6 4.5 %copy.12 = bf16[2,58,32,512]{3,2,1,0:T(8,128)(2,1)} copy(bf16[2,58,32,512]{3,2,1,0:T(8,128)(2,1)} %get-tuple-element.8) | data formatting | bytes 7602176
  57.1 0.0 copy-done
  57.1 0.7 %copy.13 = f32[2,72,512]{2,1,0:T(8,128)} copy(f32[2,72,512]{2,1,0:T(8,128)S(1)} %bitcast.5) | data formatting | bytes 589824
Async XLA Ops:
  52.6 4.5 %copy-start = (f32[144,512]{1,0:T(8,128)S(1)}, f32[144,512]{1,0:T(8,128)}, u32[]{:S(2)}) copy-start(f32[144,512]{1,0:T(8,128)} %get-tuple-element.5) | copy-start | bytes 884740

commit v2 on v1

v2 whole, which is shorter than its diff:
```python
import functools

import numpy as np
import jax
import jax.numpy as jnp
from jax import lax
from jax.experimental import pallas as pl
from jax.experimental.pallas import tpu as pltpu
from jax.sharding import PartitionSpec as P

LEV = 72
CRM_NX = 32
CRM_LEV = 58
PCOL = 4
NBR = 8
WIDTH = 128
SIDE = 64
VMEM_BYTES = 40 * 1024 * 1024
CHUNK = 256

RELAX = 0.5
STEP = 0.5
MIXING = 0.2
LATENT = 0.6
SMOOTHING = 0.5

MESH = pl.DeviceIdType.MESH
F32 = jnp.float32
BF16 = jnp.bfloat16


def interpolation(rows_out, rows_in):
    target = np.arange(rows_out, dtype=np.int32)[:, None]
    source = np.arange(rows_in, dtype=np.int32)[None, :]
    scaled = target * (rows_in - 1)
    lower = scaled // (rows_out - 1)
    weight = (scaled - lower * (rows_out - 1)).astype(np.float32) / np.float32(rows_out - 1)
    upper = np.minimum(lower + 1, rows_in - 1)
    zero = np.float32(0.0)
    return np.where(source == lower, np.float32(1.0) - weight, zero) + np.where(
        source == upper, weight, zero
    )


def interpolation_padded(rows_out, rows_in, height, width):
    matrix = np.zeros((height, width), np.float32)
    matrix[:rows_out, :rows_in] = interpolation(rows_out, rows_in)
    return matrix


def halves(values):
    high = values.astype(BF16)
    low = (values - high.astype(F32)).astype(BF16)
    return high, low


def dot(a, b, dims):
    return lax.dot_general(a, b, (dims, ((), ())), preferred_element_type=F32)


AB = ((1,), (0,))
ABT = ((1,), (1,))


def split_dot(values, chosen, dims):
    rows = values.shape[0]
    both = dot(jnp.concatenate(halves(values), axis=0), chosen, dims)
    return both[:rows] + both[rows:]


def exact_dot(a, b):
    return lax.dot_general(
        a,
        b,
        (AB, ((), ())),
        precision=lax.Precision.HIGHEST,
        preferred_element_type=F32,
    )


def onehot(mask):
    return jnp.where(mask, 1.0, 0.0).astype(BF16)


def pack(pick, values, buffer):
    devices, rows, _ = buffer.shape
    half = devices * rows
    parts = jnp.concatenate(halves(values), axis=0)
    step = min(CHUNK, half)
    lanes = lax.broadcasted_iota(jnp.int32, (step, WIDTH), 1)
    for at in range(0, half, step):
        first = dot(pick[at : at + step, :], parts, ABT)
        second = dot(pick[half + at : half + at + step, :], parts, ABT)
        first = first + pltpu.roll(first, SIDE, 1)
        second = second + pltpu.roll(second, SIDE, 1)
        folded = jnp.where(lanes < SIDE, first, second)
        buffer[at // rows : (at + step) // rows] = folded.reshape(step // rows, rows, WIDTH)


def unpack(buffer, pick):
    devices, rows, _ = buffer.shape
    turned = buffer[...].reshape(devices * rows, WIDTH).T
    return split_dot(jnp.concatenate([turned[:SIDE], turned[SIDE:]], axis=1), pick[...], AB)


def kernel(
    devices,
    gcm_hbm,
    crm_hbm,
    span_hbm,
    cost_hbm,
    near_hbm,
    down_hbm,
    up_hbm,
    next_ref,
    smooth_ref,
    gcm_ref,
    span_ref,
    cost_ref,
    near_ref,
    down_ref,
    up_ref,
    crm_buf,
    fields,
    condensed,
    pick_out,
    pick_in,
    sent,
    arrived,
    sent_back,
    arrived_back,
    start_mean,
    forcing,
    change,
    own_mean,
    near_mean,
    near_pick,
    load_sem,
    out_send,
    out_recv,
    back_send,
    back_recv,
    near_send,
    near_recv,
):
    me = lax.axis_index("cols")
    columns = gcm_ref.shape[2]
    elements = near_ref.shape[1]
    capacity = 2 * columns // devices
    rows = sent.shape[2]
    half = devices * rows
    column_bits = columns.bit_length() - 1

    barrier = pltpu.get_barrier_semaphore()

    def greet(k, carry):
        pl.semaphore_signal(
            barrier, inc=1, device_id=(lax.rem(me + k, devices),), device_id_type=MESH
        )
        return carry

    lax.fori_loop(1, devices, greet, 0)

    loads = [
        pltpu.make_async_copy(source, landing, load_sem.at[i])
        for i, (source, landing) in enumerate(
            (
                (span_hbm, span_ref),
                (gcm_hbm, gcm_ref),
                (down_hbm, down_ref),
                (cost_hbm, cost_ref),
                (crm_hbm, crm_buf.at[:, pl.ds(1, CRM_LEV)]),
                (near_hbm, near_ref),
                (up_hbm, up_ref),
            )
        )
    ]
    for load in loads:
        load.start()
    loads[0].wait()

    span = span_ref[...]
    target = lax.shift_right_logical(span, column_bits)
    place = jnp.bitwise_and(span, columns - 1)
    peers = lax.broadcasted_iota(jnp.int32, (devices, columns), 0)
    mine = peers == target
    first = lax.broadcasted_iota(jnp.int32, (columns, columns), 0)
    second = lax.broadcasted_iota(jnp.int32, (columns, columns), 1)
    before = dot(onehot(mine), onehot(first < second), AB)
    slot = before + (peers * rows).astype(F32)
    if capacity > rows:
        slot = jnp.where(before < rows, slot, slot + (half - rows))
    position = jnp.sum(jnp.where(mine, slot, 0.0), axis=0, keepdims=True).astype(jnp.int32)
    for at in range(0, 2 * half, CHUNK):
        index = lax.broadcasted_iota(jnp.int32, (CHUNK, columns), 0) + at
        pick_out[at : at + CHUNK, :] = onehot(index == position)

    row = lax.broadcasted_iota(jnp.int32, (SIDE, columns), 0)
    for load in loads[1:4]:
        load.wait()
    message = exact_dot(down_ref[...], gcm_ref[1])
    message = jnp.where(row == CRM_LEV, (place + 1).astype(F32), message)
    message = jnp.where(row == CRM_LEV + 1, cost_ref[...].astype(F32), message)
    pack(pick_out, message, sent.at[1])

    pl.semaphore_wait(barrier, devices - 1)

    def relay(source, landing, send_sem, recv_sem):
        def send(k, carry):
            peer = lax.rem(me + devices // 2 + k - 1 + (2 * k - 1) // devices, devices)
            pltpu.make_async_remote_copy(
                src_ref=source.at[peer],
                dst_ref=landing.at[me],
                send_sem=send_sem,
                recv_sem=recv_sem,
                device_id=(peer,),
                device_id_type=MESH,
            ).start()
            return carry

        lax.fori_loop(1, devices, send, 0)
        landing[me] = source[me]
        return pltpu.make_async_remote_copy(
            src_ref=source.at[pl.ds(0, devices - 1)],
            dst_ref=landing.at[pl.ds(0, devices - 1)],
            send_sem=send_sem,
            recv_sem=recv_sem,
            device_id=(lax.rem(me + 1, devices),),
            device_id_type=MESH,
        )

    outward = [None, relay(sent.at[1], arrived.at[1], out_send.at[1], out_recv.at[1])]
    pack(pick_out, exact_dot(down_ref[...], gcm_ref[0]), sent.at[0])
    outward[0] = relay(sent.at[0], arrived.at[0], out_send.at[0], out_recv.at[0])

    for load in loads[4:]:
        load.wait()
    for field in range(2):
        crm_buf[field, 0] = crm_buf[field, 1]
        crm_buf[field, CRM_LEV + 1] = crm_buf[field, CRM_LEV]

    def stencil(here, above, below):
        sideways = pltpu.roll(here, 1, 0) + pltpu.roll(here, CRM_NX - 1, 0)
        return here + (STEP * MIXING) * ((sideways + (above + below)) - 4.0 * here)

    for field in (1, 0):

        def prepare(j, carry, field=field):
            here = crm_buf[field, j + 1].astype(F32)
            above = crm_buf[field, j + 2].astype(F32)
            below = crm_buf[field, j].astype(F32)
            fields[field, j + 1] = stencil(here, above, below)
            start_mean[field, pl.ds(j, 1), :] = jnp.sum(here, axis=0, keepdims=True) * (
                1.0 / CRM_NX
            )
            return carry

        start_mean[field, CRM_LEV:, :] = jnp.zeros((SIDE - CRM_LEV, columns), F32)
        change[field, CRM_LEV:, :] = jnp.zeros((SIDE - CRM_LEV, columns), F32)
        lax.fori_loop(0, CRM_LEV, prepare, 0)

    near = near_ref[...]
    total = devices * elements
    offset = near - (me - 1) * elements
    offset = jnp.where(offset < 0, offset + total, offset)
    offset = jnp.where(offset >= total, offset - total, offset)
    offset = jnp.where(near >= 0, offset, -1)
    spots = lax.broadcasted_iota(jnp.int32, (3 * elements, elements), 0)
    chosen = jnp.zeros((3 * elements, elements), F32)
    for s in range(NBR):
        chosen = chosen + jnp.where(offset[s : s + 1, :] == spots, 1.0, 0.0)
    near_pick[...] = chosen.astype(BF16)
    count = jnp.sum(chosen, axis=0, keepdims=True)
    scale = 1.0 / count

    outward[1].wait_recv()
    landed = arrived[1].reshape(half, WIDTH)
    columns_at = lax.broadcasted_iota(jnp.int32, (half, columns), 1) + 1
    for side in range(2):
        lane = side * SIDE + CRM_LEV
        labels = landed[:, lane : lane + 1].astype(jnp.int32)
        pick_in[side * half : (side + 1) * half, :] = onehot(labels == columns_at)

    def force(field):
        placed = unpack(arrived.at[field], pick_in)
        forcing[field] = (STEP * RELAX) * (placed - start_mean[field])
        return placed

    def close(field):
        fields[field, 0] = fields[field, 1]
        fields[field, CRM_LEV + 1] = fields[field, CRM_LEV]

    def finish(field, j, final):
        next_ref[field, j] = final.astype(BF16)
        at = pl.ds(j, 1)
        change[field, at, :] = (
            jnp.sum(final, axis=0, keepdims=True) * (1.0 / CRM_NX) - start_mean[field, at, :]
        )

    def send_back(field):
        pack(pick_in, change[field], sent_back.at[field])
        return relay(
            sent_back.at[field], arrived_back.at[field], back_send.at[field], back_recv.at[field]
        )

    top = force(1)[CRM_LEV + 1 : CRM_LEV + 2, :]

    def condense(j, step, moisture):
        level = j.astype(F32)
        saturation = 1.0 - 0.8 * level / (CRM_LEV - 1)
        active = jnp.where(level < top, 1.0, 0.0)
        taken = jnp.maximum(moisture - saturation, 0.0) * active
        condensed[step, j] = taken
        return moisture - taken

    def first_moisture(j, carry):
        moisture = fields[1, j + 1] + forcing[1, pl.ds(j, 1), :]
        fields[1, j + 1] = condense(j, 0, moisture)
        return carry

    lax.fori_loop(0, CRM_LEV, first_moisture, 0)
    close(1)

    def second_moisture(j, carry):
        moisture = stencil(fields[1, j + 1], fields[1, j + 2], fields[1, j])
        finish(1, j, condense(j, 1, moisture + forcing[1, pl.ds(j, 1), :]))
        return carry

    lax.fori_loop(0, CRM_LEV, second_moisture, 0)
    inward = [None, send_back(1)]

    outward[0].wait_recv()
    force(0)

    def first_heat(j, carry):
        fields[0, j + 1] = fields[0, j + 1] + forcing[0, pl.ds(j, 1), :] + LATENT * condensed[0, j]
        return carry

    lax.fori_loop(0, CRM_LEV, first_heat, 0)
    close(0)

    def second_heat(j, carry):
        heat = stencil(fields[0, j + 1], fields[0, j + 2], fields[0, j])
        finish(0, j, heat + forcing[0, pl.ds(j, 1), :] + LATENT * condensed[1, j])
        return carry

    lax.fori_loop(0, CRM_LEV, second_heat, 0)
    inward[0] = send_back(0)

    member = lax.broadcasted_iota(jnp.int32, (elements, columns), 1)
    lowest = lax.broadcasted_iota(jnp.int32, (elements, columns), 0) * PCOL
    inside = onehot((member >= lowest) & (member < lowest + PCOL))
    exchanges = [[], []]
    for field in (1, 0):
        inward[field].wait_recv()
        updated = gcm_ref[field] + exact_dot(up_ref[...], unpack(arrived_back.at[field], pick_out))
        smooth_ref[field] = updated
        own_mean[field] = split_dot(updated, inside, ABT) * (1.0 / PCOL)
        for side in range(2):
            peer = lax.rem(me + 1, devices) if side == 0 else lax.rem(me + devices - 1, devices)
            exchange = pltpu.make_async_remote_copy(
                src_ref=own_mean.at[field],
                dst_ref=near_mean.at[field, side],
                send_sem=near_send.at[field, side],
                recv_sem=near_recv.at[field, side],
                device_id=(peer,),
                device_id_type=MESH,
            )
            exchange.start()
            exchanges[field].append(exchange)
    for field in (1, 0):
        edge_mean = own_mean[field]
        around = split_dot(edge_mean, near_pick[elements : 2 * elements, :], AB)
        for side in range(2):
            exchanges[field][side].wait_recv()
            spot = 2 * side * elements
            around = around + split_dot(
                near_mean[field, side], near_pick[spot : spot + elements, :], AB
            )
        pull = SMOOTHING * (around * scale - edge_mean)
        smooth_ref[field] = smooth_ref[field] + split_dot(pull, inside, AB)

    for field in (1, 0):
        outward[field].wait_send()
        inward[field].wait_send()
        for exchange in exchanges[field]:
            exchange.wait_send()


def on_device(devices, gcm_state, crm_state, span_map, crm_cost, neighbours):
    columns = gcm_state.shape[2]
    elements = neighbours.shape[0]
    rows = max(8, columns // devices)
    slots = 2 * devices * rows
    down = jnp.asarray(interpolation_padded(CRM_LEV, LEV, SIDE, LEV))
    up = jnp.asarray(interpolation_padded(LEV, CRM_LEV, LEV, SIDE))
    vmem = pl.BlockSpec(memory_space=pltpu.VMEM)
    hbm = pl.BlockSpec(memory_space=pltpu.HBM)
    relay = pltpu.VMEM((2, devices, rows, WIDTH), F32)
    per_level = pltpu.VMEM((2, SIDE, columns), F32)
    pair = pltpu.SemaphoreType.DMA((2,))
    crm_next, smoothed = pl.pallas_call(
        functools.partial(kernel, devices),
        out_shape=(
            jax.ShapeDtypeStruct(crm_state.shape, BF16),
            jax.ShapeDtypeStruct((2, LEV, columns), F32),
        ),
        in_specs=[hbm] * 7,
        out_specs=(vmem, vmem),
        scratch_shapes=[
            pltpu.VMEM((2, LEV, columns), F32),
            pltpu.VMEM((1, columns), jnp.int32),
            pltpu.VMEM((1, columns), jnp.int32),
            pltpu.VMEM((NBR, elements), jnp.int32),
            pltpu.VMEM((SIDE, LEV), F32),
            pltpu.VMEM((LEV, SIDE), F32),
            pltpu.VMEM((2, CRM_LEV + 2, CRM_NX, columns), BF16),
            pltpu.VMEM((2, CRM_LEV + 2, CRM_NX, columns), F32),
            pltpu.VMEM((2, CRM_LEV, CRM_NX, columns), F32),
            pltpu.VMEM((slots, columns), BF16),
            pltpu.VMEM((slots, columns), BF16),
            relay,
            relay,
            relay,
            relay,
            per_level,
            per_level,
            per_level,
            pltpu.VMEM((2, LEV, elements), F32),
            pltpu.VMEM((2, 2, LEV, elements), F32),
            pltpu.VMEM((3 * elements, elements), BF16),
            pltpu.SemaphoreType.DMA((7,)),
            pair,
            pair,
            pair,
            pair,
            pltpu.SemaphoreType.DMA((2, 2)),
            pltpu.SemaphoreType.DMA((2, 2)),
        ],
        compiler_params=pltpu.CompilerParams(
            collective_id=0, has_side_effects=True, vmem_limit_bytes=VMEM_BYTES
        ),
    )(
        *(
            pltpu.with_memory_space_constraint(x, pltpu.HBM)
            for x in (
                gcm_state,
                crm_state,
                span_map.reshape(1, columns),
                crm_cost.reshape(1, columns),
                neighbours.T,
                down,
                up,
            )
        )
    )
    return crm_next, smoothed


def solution(mesh):
    placed = (
        P(None, None, "cols"),
        P(None, None, None, "cols"),
        P("cols"),
        P("cols"),
        P("cols", None),
    )
    return jax.shard_map(
        functools.partial(on_device, mesh.shape["cols"]),
        mesh=mesh,
        in_specs=placed,
        out_specs=(P(None, None, None, "cols"), P(None, None, "cols")),
        check_vma=False,
    )
```

time: 58 us -> 44.5 us (0.77)
  the two profiles are of different devices: /device:TPU:0 before, /device:TPU:1 now
where the time goes in v2:
time: 44.5 us; the launch traced here: 44.3 us
  Pallas kernels  41.1 us (92%)
  local copies, waits for them, and re-layouts  2.6 us (6%)
  between operations  0.64 us (1%)
    pallas_call x1, Pallas kernels, on_device(): pl.pallas_call(functools.partial(kernel, devices), out_shape=(jax.ShapeDt...  41.1 us
    unnamed x2, local copies, waits for them, and re-layouts  2.6 us

profile of v2, /device:TPU:1, one launch (start us, length us, event | category | flops | bytes accessed | tf_op | source)
XLA Modules:
  0.0 44.3 jit_solution(16584729781848460576)
XLA Ops:
  0.6 41.1 %shard_map.86 = (bf16[2,58,32,512]{3,2,1,0:T(8,128)(2,1)S(1)}, f32[2,72,512]{2,1,0:T(8,128)S(1)}) custom-call(f32[2,72,512]{2,1,0:T(8,128)} %gcm_hbm.1, bf16[2,58,32,512]{3,2,1,0:T(8,128)(2,1)} %crm_hbm.1, s32[1,512]{1,0:T(1,128)} %bitcast.4, s32[1,512]{1,0:T(1,128)} %bitcast.5, s32[8,128]{1,0:T(8,128)} %bitcast.3, f32[64,72]{1,0:T(8,128)} %constant.4.clone.down_hbm, ...), custom_call_target="tpu_custom_call" | custom-call | tf_op jit(solution)/shard_map/pallas_call | solution.py:402
  41.7 1.9 %copy.11 = bf16[2,58,32,512]{3,2,1,0:T(8,128)(2,1)} copy(bf16[2,58,32,512]{3,2,1,0:T(8,128)(2,1)S(1)} %get-tuple-element.4) | data formatting | bytes 7602176
  43.6 0.7 %copy.12 = f32[2,72,512]{2,1,0:T(8,128)} copy(f32[2,72,512]{2,1,0:T(8,128)S(1)} %get-tuple-element.5) | data formatting | bytes 589824

commit v3 on v2

--- a/solution.py
+++ b/solution.py
@@ -352,10 +352,11 @@
     inside = onehot((member >= lowest) & (member < lowest + PCOL))
     exchanges = [[], []]
     for field in (1, 0):
+        still_mean = split_dot(gcm_ref[field], inside, ABT)
         inward[field].wait_recv()
-        updated = gcm_ref[field] + exact_dot(up_ref[...], unpack(arrived_back.at[field], pick_out))
-        smooth_ref[field] = updated
-        own_mean[field] = split_dot(updated, inside, ABT) * (1.0 / PCOL)
+        own = unpack(arrived_back.at[field], pick_out)
+        moved = exact_dot(up_ref[...], split_dot(own, inside, ABT))
+        own_mean[field] = (still_mean + moved) * (1.0 / PCOL)
         for side in range(2):
             peer = lax.rem(me + 1, devices) if side == 0 else lax.rem(me + devices - 1, devices)
             exchange = pltpu.make_async_remote_copy(
@@ -368,6 +369,7 @@
             )
             exchange.start()
             exchanges[field].append(exchange)
+        smooth_ref[field] = gcm_ref[field] + exact_dot(up_ref[...], own)
     for field in (1, 0):
         edge_mean = own_mean[field]
         around = split_dot(edge_mean, near_pick[elements : 2 * elements, :], AB)

time: 44.5 us -> 44.4 us (level)
  no operation moved by 1% of the time
where the time goes in v3:
time: 44.4 us; the launch traced here: 44.2 us
  Pallas kernels  41 us (92%)
  local copies, waits for them, and re-layouts  2.6 us (6%)
  between operations  0.64 us (1%)
    pallas_call x1, Pallas kernels, on_device(): pl.pallas_call(functools.partial(kernel, devices), out_shape=(jax.ShapeDt...  41 us
    unnamed x2, local copies, waits for them, and re-layouts  2.6 us

profile of v3, /device:TPU:1, one launch (start us, length us, event | category | flops | bytes accessed | tf_op | source)
XLA Modules:
  0.0 44.2 jit_solution(10586421940928888359)
XLA Ops:
  0.6 41.0 %shard_map.86 = (bf16[2,58,32,512]{3,2,1,0:T(8,128)(2,1)S(1)}, f32[2,72,512]{2,1,0:T(8,128)S(1)}) custom-call(f32[2,72,512]{2,1,0:T(8,128)} %gcm_hbm.1, bf16[2,58,32,512]{3,2,1,0:T(8,128)(2,1)} %crm_hbm.1, s32[1,512]{1,0:T(1,128)} %bitcast.4, s32[1,512]{1,0:T(1,128)} %bitcast.5, s32[8,128]{1,0:T(8,128)} %bitcast.3, f32[64,72]{1,0:T(8,128)} %constant.4.clone.down_hbm, ...), custom_call_target="tpu_custom_call" | custom-call | tf_op jit(solution)/shard_map/pallas_call | solution.py:404
  41.6 1.9 %copy.11 = bf16[2,58,32,512]{3,2,1,0:T(8,128)(2,1)} copy(bf16[2,58,32,512]{3,2,1,0:T(8,128)(2,1)S(1)} %get-tuple-element.4) | data formatting | bytes 7602176
  43.5 0.7 %copy.12 = f32[2,72,512]{2,1,0:T(8,128)} copy(f32[2,72,512]{2,1,0:T(8,128)S(1)} %get-tuple-element.5) | data formatting | bytes 589824
